TPU v7x, 32 devices: a whole 2x2x4 slice. The times are simulated.
32 devices in a mesh: row: 8 (over z, x), col: 4 (over y, core).
Axes of the slice: x: 2, y: 2, z: 4, core: 2. Of those that a mesh axis runs over, the one named last changes fastest.
Arguments:
- solution_field: float32 [32, 32768], P(None, ('row', 'col')), may hold values from -6 to 6
- residual: float32 [32, 32768], P(None, ('row', 'col')), may hold values from -420 to 420
- direction: float32 [32, 32768], P(None, ('row', 'col')), may hold values from -420 to 420
- positions: bfloat16 [2, 32768], P(None, ('row', 'col')), may hold values from -6 to 6
- tile_pairs: int32 [2, 49152], P(None, ('row', 'col')), may hold values from 0 to 63, as said below
- pair_count: int32 [32], P(('row', 'col')), may hold values from 0 to 1536, as said below
Outputs:
- solution_next: float32 [32, 32768], P(None, ('row', 'col'))
- residual_next: float32 [32, 32768], P(None, ('row', 'col'))
- direction_next: float32 [32, 32768], P(None, ('row', 'col'))
Inputs may be any that keep to these rules, and one draw needn't show every extreme that they name: `tile_pairs`: row 0 holds local row tiles below 32, row 1 local column tiles below 64. The live pairs of one slot block are distinct and strictly upper (I < J); entries in slots that are not live are in range but carry nothing. `pair_count`: some slot block is full in every draw.
All inputs are finite; a program needn't handle non-finite values.
Results may differ from a plain program's by a relative error of at most 0.007.
Values may be sent and summed in bfloat16 or wider, within the bound.
A program may use at most 64 MiB of HBM per device.

v0:
```python
import math
import jax
import jax.numpy as jnp
from jax import lax
from jax.sharding import PartitionSpec as P

TILE = 128
AMPLITUDE = 0.025
NUGGET = 2.0
RADIUS = 1.0
HIGHEST = lax.Precision.HIGHEST


def kernel_tile(near_side, far_side):
    differ = near_side[..., :, None] - far_side[..., None, :]
    distance = jnp.sqrt(jnp.sum(differ * differ, axis=0)) / RADIUS
    remain = jnp.maximum(1.0 - distance, 0.0)
    return AMPLITUDE * remain**4 * (4.0 * distance + 1.0)


def cross_gram_matrix(former, latter):
    return lax.dot_general(
        former,
        latter,
        (((1,), (1,)), ((), ())),
        precision=HIGHEST,
        preferred_element_type=jnp.float32,
    )


def apply_left(matrix, vectors):
    return jnp.dot(matrix.T, vectors, precision=HIGHEST)


def symmetric_solve(matrix, target):
    balanced = 0.5 * (matrix + matrix.T)
    factor = jnp.linalg.cholesky(balanced)
    middle = lax.linalg.triangular_solve(factor, target, left_side=True, lower=True)
    return lax.linalg.triangular_solve(factor, middle, left_side=True, lower=True, transpose_a=True)


def on_device(solution_field, residual, direction, positions, tile_pairs, pair_count):
    probes, own_points = direction.shape
    own_tiles = own_points // TILE
    dir_half = direction.astype(jnp.bfloat16)
    row_dir, row_pos = (
        lax.all_gather(dir_half, "col", axis=1, tiled=True),
        lax.all_gather(positions, "col", axis=1, tiled=True),
    )
    col_dir, col_pos = (
        lax.all_gather(dir_half, "row", axis=1, tiled=True),
        lax.all_gather(positions, "row", axis=1, tiled=True),
    )
    own_pos = positions.astype(jnp.float32).reshape(2, own_tiles, TILE)
    diagonal = kernel_tile(own_pos, own_pos).astype(jnp.bfloat16)
    own_product = jnp.einsum(
        "npq,knq->knp",
        diagonal,
        dir_half.reshape(probes, own_tiles, TILE),
        preferred_element_type=jnp.float32,
    ).reshape(probes, own_points)
    row_tiles = row_dir.shape[1] // TILE
    col_tiles = col_dir.shape[1] // TILE
    row_vector = row_dir.reshape(probes, row_tiles, TILE)
    column_vector = col_dir.reshape(probes, col_tiles, TILE)
    row_coord = row_pos.reshape(2, row_tiles, TILE)
    col_coord = col_pos.reshape(2, col_tiles, TILE)
    row_range = jnp.arange(row_tiles, dtype=jnp.int32)
    col_range = jnp.arange(col_tiles, dtype=jnp.int32)
    slot_total = tile_pairs.shape[1]
    block_size = math.gcd(slot_total, 64)
    live_count = pair_count[0]

    def stepped(block_no, running_totals):
        row_acc, col_acc = running_totals
        first_slot = block_no * block_size
        row_index = lax.dynamic_slice_in_dim(tile_pairs[0], first_slot, block_size)
        col_index = lax.dynamic_slice_in_dim(tile_pairs[1], first_slot, block_size)
        live_mask = first_slot + jnp.arange(block_size, dtype=jnp.int32) < live_count
        row_chosen_index = (row_index[:, None] == row_range[None, :]).astype(jnp.bfloat16)
        column_chosen_index = (col_index[:, None] == col_range[None, :]).astype(jnp.bfloat16)
        near_side = jnp.einsum(
            "bt,ctq->cbq", row_chosen_index, row_coord, preferred_element_type=jnp.float32
        )
        far_side = jnp.einsum(
            "bt,ctq->cbq", column_chosen_index, col_coord, preferred_element_type=jnp.float32
        )
        row_sel = jnp.einsum(
            "di,siz->sdz", row_chosen_index, row_vector, preferred_element_type=jnp.float32
        ).astype(jnp.bfloat16)
        col_sel = jnp.einsum(
            "di,siz->sdz", column_chosen_index, column_vector, preferred_element_type=jnp.float32
        ).astype(jnp.bfloat16)
        kernel_block = kernel_tile(near_side, far_side)
        kernel_block = jnp.where(live_mask[:, None, None], kernel_block, 0.0).astype(jnp.bfloat16)
        forward_step = jnp.einsum(
            "bpq,kbq->kbp", kernel_block, col_sel, preferred_element_type=jnp.float32
        )
        backward = jnp.einsum(
            "bpq,kbp->kbq", kernel_block, row_sel, preferred_element_type=jnp.float32
        )
        row_add = jnp.einsum(
            "bt,kbp->ktp",
            row_chosen_index.astype(jnp.float32),
            forward_step,
            precision=HIGHEST,
            preferred_element_type=jnp.float32,
        )
        col_add = jnp.einsum(
            "au,lax->lux",
            column_chosen_index.astype(jnp.float32),
            backward,
            precision=HIGHEST,
            preferred_element_type=jnp.float32,
        )
        return (row_acc + row_add, col_acc + col_add)

    start_totals = (
        jnp.zeros((probes, row_tiles, TILE), jnp.float32),
        jnp.zeros((probes, col_tiles, TILE), jnp.float32),
    )
    row_acc, col_acc = lax.fori_loop(0, slot_total // block_size, stepped, start_totals)
    row_flat = row_acc.reshape(probes, row_tiles * TILE)
    col_flat = col_acc.reshape(probes, col_tiles * TILE)
    row_whole = lax.psum(row_flat.astype(jnp.bfloat16), "col").astype(jnp.float32)
    row_part = lax.dynamic_slice_in_dim(
        row_whole, lax.axis_index("col") * own_points, own_points, 1
    )
    col_whole = lax.psum(col_flat.astype(jnp.bfloat16), "row").astype(jnp.float32)
    col_part = lax.dynamic_slice_in_dim(
        col_whole, lax.axis_index("row") * own_points, own_points, 1
    )
    applied = NUGGET * direction + own_product + row_part + col_part
    curvature, crossing, norm_old, image_resid, square = lax.psum(
        (
            cross_gram_matrix(direction, applied),
            cross_gram_matrix(direction, residual),
            cross_gram_matrix(residual, residual),
            cross_gram_matrix(applied, residual),
            cross_gram_matrix(applied, applied),
        ),
        ("row", "col"),
    )
    step_size = symmetric_solve(curvature, crossing)
    residual_next = residual - apply_left(step_size, applied)
    shifted = jnp.dot(step_size.T, image_resid, precision=HIGHEST)
    quadratic = jnp.dot(
        step_size.T, jnp.dot(square, step_size, precision=HIGHEST), precision=HIGHEST
    )
    norm_new = norm_old - shifted - shifted.T + quadratic
    solution_next = solution_field + apply_left(step_size, direction)
    mix_weight = symmetric_solve(norm_old, norm_new)
    direction_next = residual_next + apply_left(mix_weight, direction)
    return (solution_next, residual_next, direction_next)


def solution(mesh):
    in_specs = (
        P(None, ("row", "col")),
        P(None, ("row", "col")),
        P(None, ("row", "col")),
        P(None, ("row", "col")),
        P(None, ("row", "col")),
        P(("row", "col")),
    )
    out_specs = (P(None, ("row", "col")), P(None, ("row", "col")), P(None, ("row", "col")))
    return jax.shard_map(
        on_device, mesh=mesh, in_specs=in_specs, out_specs=out_specs, check_vma=False
    )
```

profile of v0, /device:TPU:0, one launch (start us, length us, event | category | flops | bytes accessed | tf_op | source)
XLA Modules:
  0.0 675.7 jit_solution(7881946723567846366)
XLA Ops:
  8.1 33.0 %all_gather.12 = bf16[32,8192]{1,0:T(8,128)(2,1)S(1)} all-gather(bf16[32,1024]{1,0:T(8,128)(2,1)S(1)} %convert_element_type.65), channel_id=1, replica_groups=mesh['row'=8,'col'=4] {'row'}, dimensions={1}, use_global_device_ids=true | all-gather | bytes 589824 | tf_op jit(solution)/shard_map/all_gather | solution.py:51
  41.2 5.8 all_gather.15
  46.9 30.7 %all_gather.14 = bf16[2,8192]{1,0:T(2,128)(2,1)S(1)} all-gather(bf16[2,1024]{1,0:T(2,128)(2,1)} %param.16), channel_id=1, replica_groups=mesh['row'=8,'col'=4] {'row'}, dimensions={1}, use_global_device_ids=true | all-gather | bytes 36864 | tf_op jit(solution)/shard_map/all_gather | solution.py:52
  77.7 5.3 all_gather.13
  84.0 413.3 %while.16 = (s32[]{:T(128)}, f32[32,32,128]{2,1,0:T(8,128)}, f32[32,64,128]{2,1,0:T(8,128)}, s32[2,1536]{1,0:T(2,128)}, bf16[32,64,128]{2,1,0:T(8,128)(2,1)}, /*...) while((s32[]{:T(128)}, f32[32,32,128]{2,1,0:T(8,128)}, ...), condition=%wide.region_3.4_spmd.clone, body=%wide.region_1.3_spmd.clone.sunk | while | flops 506742912 | bytes 25242432 | solution.py:122
  107.3 3.5 fusion.128
  113.4 3.0 fusion.126
  124.6 3.5 fusion.128
  130.7 3.0 fusion.126
  141.9 3.5 fusion.128
  148.1 3.0 fusion.126
  159.2 3.5 fusion.128
  165.4 3.0 fusion.126
  176.5 3.5 fusion.128
  182.7 3.0 fusion.126
  193.9 3.5 fusion.128
  200.0 3.0 fusion.126
  211.2 3.5 fusion.128
  217.3 3.0 fusion.126
  228.5 3.5 fusion.128
  234.6 3.0 fusion.126
  245.8 3.5 fusion.128
  263.1 3.5 fusion.128
  269.3 3.0 fusion.126
  280.4 3.5 fusion.128
  286.6 3.0 fusion.126
  297.7 3.5 fusion.128
  303.9 3.0 fusion.126
  315.1 3.5 fusion.128
  332.4 3.5 fusion.128
  349.7 3.5 fusion.128
  355.8 3.0 fusion.126
  367.0 3.5 fusion.128
  373.1 3.0 fusion.126
  384.3 3.5 fusion.128
  390.5 3.0 fusion.126
  401.6 3.5 fusion.128
  418.9 3.5 fusion.128
  436.2 3.5 fusion.128
  442.4 3.0 fusion.126
  453.6 3.5 fusion.128
  459.7 3.0 fusion.126
  470.9 3.5 fusion.128
  477.0 3.0 fusion.126
  488.2 3.5 fusion.128
  503.2 29.6 %all-reduce.4.cloned.1.call-done = bf16[32,4096]{1,0:T(8,128)(2,1)} async-done(((bf16[32,4096]{1,0:T(8,128)(2,1)}), bf16[32,4096]{1,0:T(8,128)(2,1)}) %all-reduce.4.cloned.1.call-update) | async-done | bytes 262160 | tf_op jit(solution)/shard_map/psum | solution.py:125
  532.8 76.2 %all-reduce.6.cloned.1.call-done = bf16[32,8192]{1,0:T(8,128)(2,1)} async-done(((bf16[32,8192]{1,0:T(8,128)(2,1)}), bf16[32,8192]{1,0:T(8,128)(2,1)}) %all-reduce.6.cloned.1.call-update) | async-done | bytes 524304 | tf_op jit(solution)/shard_map/psum | solution.py:129
  610.7 40.8 %all-reduce = (f32[32,32]{1,0:T(8,128)S(1)}, f32[32,32]{1,0:T(8,128)S(1)}, f32[32,32]{1,0:T(8,128)S(1)}, f32[32,32]{1,0:T(8,128)S(1)}, f32[32,32]{1,0:T(8,128)S(1)}) all-reduce(f32[32,32]{1,0:T(8,128)S(1)} %fusion.49, f32[32,32]{1,0:T(8,128)S(1)} %convolution_bitcast_fusion.7, ...), channel_id=1, replica_groups=mesh['row'=8,'col'=4] {'row','col'}, use_global_device_ids=true, to_apply=%region_9.0 | all-reduce | flops 5120 | bytes 40960 | tf_op jit(solution)/shard_map/psum | solution.py:134
  (335 shorter events, 306.9 us)
Async XLA Ops:
  7.2 525.6 %all-reduce.4.cloned.1.call-start = ((), (), s32[]{:S(2)}) async-start(), calls=%async_computation | async-start | bytes 524288 | tf_op jit(solution)/shard_map/psum | solution.py:125
  497.3 4.6 copy-start.4
  497.3 4.9 copy-start
  497.3 5.3 copy-start.1
  499.3 167.7 %copy-start.3 = (f32[32,1024]{1,0:T(8,128)S(1)}, f32[32,1024]{1,0:T(8,128)}, u32[]{:S(2)}) copy-start(f32[32,1024]{1,0:T(8,128)} %param.13) | copy-start | bytes 393220
  499.3 109.7 %all-reduce.6.cloned.1.call-start = ((), (), s32[]{:S(2)}) async-start(), calls=%async_computation.1 | async-start | bytes 1048576 | tf_op jit(solution)/shard_map/psum | solution.py:129
  665.9 3.0 copy-start.2
Sparse Core Ops, SparseCore 0:
  499.4 33.3 all-reduce.3
  536.2 72.7 all-reduce.5
where the time goes:
time: 681 us; the launch traced here: 676 us
  matrix products  255 us (37%)
  other arithmetic  159 us (23%)
  blocking collectives  116 us (17%)
  waiting for transfers between devices  106 us (16%)
  local copies, waits for them, and re-layouts  24.3 us (4%)
  between operations  14.3 us (2%)
    dot_general x24, matrix products, stepped(): jnp.einsum('au,lax->lux', column_chosen_index.astype(jnp.float32), backwa...  83.6 us
    psum x1, waiting for transfers between devices, on_device(): lax.psum(col_flat.astype(jnp.bfloat16), 'row').astype(jnp.float32)  76.2 us
    dot_general x24, matrix products, stepped(): jnp.einsum('bt,kbp->ktp', row_chosen_index.astype(jnp.float32), forward_s...  70.3 us
    reduce_sum x25, other arithmetic, kernel_tile(): distance = jnp.sqrt(jnp.sum(differ * differ, axis=0)) / RADIUS  66.6 us
    convert_element_type x24, other arithmetic, stepped(): jnp.where(live_mask[:, None, None], kernel_block, 0.0).astype(jnp.bfloat16)  59 us
    psum x1, blocking collectives, on_device(): lax.psum((cross_gram_matrix(direction, applied), cross_gram_matrix(direct...  40.8 us
    dot_general x24, matrix products, stepped(): jnp.einsum('di,siz->sdz', column_chosen_index, column_vector, preferred_e...  33.2 us
    all_gather x1, blocking collectives, on_device(): lax.all_gather(dir_half, 'row', axis=1, tiled=True)  33 us
  transfers between devices with their start and end apart: 2, of which 2 were waited for; matrix products, arithmetic and copies ran while one was open for 1% of the time, Pallas kernels for 0%

commit v1 on v0

--- a/solution.py
+++ b/solution.py
@@ -9,6 +9,7 @@
 NUGGET = 2.0
 RADIUS = 1.0
 HIGHEST = lax.Precision.HIGHEST
+render_the_routes_all = lambda sample: jnp.sum(lax.all_gather(sample, "row"), 0)
 
 
 def kernel_tile(near_side, far_side):
@@ -126,7 +127,7 @@
     row_part = lax.dynamic_slice_in_dim(
         row_whole, lax.axis_index("col") * own_points, own_points, 1
     )
-    col_whole = lax.psum(col_flat.astype(jnp.bfloat16), "row").astype(jnp.float32)
+    col_whole = render_the_routes_all(col_flat.astype(jnp.bfloat16)).astype(jnp.float32)
     col_part = lax.dynamic_slice_in_dim(
         col_whole, lax.axis_index("row") * own_points, own_points, 1
     )

time: 681 us -> 657 us (0.965)
  waiting for transfers between devices: 106 us -> 70.6 us
  local copies, waits for them, and re-layouts: 24.3 us -> 31.8 us
    psum x1 -> x0, waiting for transfers between devices: 76.2 us -> none  [on_device(): lax.psum(col_flat.astype(jnp.bfloat16), 'row').astype(jnp.float32)]
    all_gather x0 -> x1, waiting for transfers between devices: none -> 70.6 us  [lax.all_gather(sample, 'row')]
    psum x1, waiting for transfers between devices: 29.6 us -> 0.03 us  [on_device(): lax.psum(row_flat.astype(jnp.bfloat16), 'col').astype(jnp.float32)]
    while x0 -> x288, local copies, waits for them, and re-layouts: none -> 7.61 us
  transfers between devices with their start and end apart: 2 -> 2, of which waited for: 2 -> 1; matrix products, arithmetic and copies ran while one was open for 1% -> 1% of each run, Pallas kernels for 0% -> 0%
where the time goes in v1:
time: 657 us; the launch traced here: 652 us
  matrix products  255 us (39%)
  other arithmetic  162 us (25%)
  blocking collectives  115 us (18%)
  waiting for transfers between devices  70.6 us (11%)
  local copies, waits for them, and re-layouts  31.8 us (5%)
  between operations  15.8 us (2%)
    dot_general x24, matrix products, stepped(): jnp.einsum('au,lax->lux', column_chosen_index.astype(jnp.float32), backwa...  83.6 us
    all_gather x1, waiting for transfers between devices, lax.all_gather(sample, 'row')  70.6 us
    dot_general x24, matrix products, stepped(): jnp.einsum('bt,kbp->ktp', row_chosen_index.astype(jnp.float32), forward_s...  69.9 us
    reduce_sum x25, other arithmetic, kernel_tile(): distance = jnp.sqrt(jnp.sum(differ * differ, axis=0)) / RADIUS  66.6 us
    convert_element_type x24, other arithmetic, stepped(): jnp.where(live_mask[:, None, None], kernel_block, 0.0).astype(jnp.bfloat16)  59 us
    psum x1, blocking collectives, on_device(): lax.psum((cross_gram_matrix(direction, applied), cross_gram_matrix(direct...  40 us
    dot_general x24, matrix products, stepped(): jnp.einsum('di,siz->sdz', column_chosen_index, column_vector, preferred_e...  33.4 us
    all_gather x1, blocking collectives, on_device(): lax.all_gather(dir_half, 'row', axis=1, tiled=True)  33 us
  transfers between devices with their start and end apart: 2, of which 1 were waited for; matrix products, arithmetic and copies ran while one was open for 1% of the time, Pallas kernels for 0%

profile of v1, /device:TPU:0, one launch (start us, length us, event | category | flops | bytes accessed | tf_op | source)
XLA Modules:
  0.0 652.1 jit_solution(2233217710417401986)
XLA Ops:
  9.0 33.0 %all_gather.16 = bf16[32,8192]{1,0:T(8,128)(2,1)S(1)} all-gather(bf16[32,1024]{1,0:T(8,128)(2,1)S(1)} %convert_element_type.74), channel_id=1, replica_groups=mesh['row'=8,'col'=4] {'row'}, dimensions={1}, use_global_device_ids=true | all-gather | bytes 589824 | tf_op jit(solution)/shard_map/all_gather | solution.py:52
  42.0 5.8 all_gather.19
  47.8 30.7 %all_gather.18 = bf16[2,8192]{1,0:T(2,128)(2,1)S(1)} all-gather(bf16[2,1024]{1,0:T(2,128)(2,1)} %param.16), channel_id=1, replica_groups=mesh['row'=8,'col'=4] {'row'}, dimensions={1}, use_global_device_ids=true | all-gather | bytes 36864 | tf_op jit(solution)/shard_map/all_gather | solution.py:53
  78.5 5.3 all_gather.17
  84.8 421.4 %while.16 = (s32[]{:T(128)}, f32[32,32,128]{2,1,0:T(8,128)}, f32[32,64,128]{2,1,0:T(8,128)}, s32[2,1536]{1,0:T(2,128)}, bf16[32,64,128]{2,1,0:T(8,128)(2,1)}, /*...) while((s32[]{:T(128)}, f32[32,32,128]{2,1,0:T(8,128)}, ...), condition=%wide.region_3.4_spmd.clone, body=%wide.region_1.3_spmd.clone.sunk | while | flops 506742912 | bytes 25508840 | solution.py:123
  108.8 3.5 fusion.128
  114.9 3.0 fusion.126
  126.4 3.5 fusion.128
  132.6 3.0 fusion.126
  144.1 3.5 fusion.128
  150.2 3.0 fusion.126
  161.7 3.5 fusion.128
  167.9 3.0 fusion.126
  179.4 3.5 fusion.128
  185.5 3.0 fusion.126
  197.0 3.5 fusion.128
  214.7 3.5 fusion.128
  220.8 3.0 fusion.126
  232.3 3.5 fusion.128
  238.5 3.0 fusion.126
  250.0 3.5 fusion.128
  256.1 3.0 fusion.126
  267.6 3.5 fusion.128
  273.8 3.0 fusion.126
  285.3 3.5 fusion.128
  291.4 3.0 fusion.126
  302.9 3.5 fusion.128
  309.1 3.0 fusion.126
  320.6 3.5 fusion.128
  338.2 3.5 fusion.128
  344.4 3.0 fusion.126
  355.9 3.5 fusion.128
  362.1 3.0 fusion.126
  373.5 3.5 fusion.128
  391.2 3.5 fusion.128
  397.4 3.0 fusion.126
  408.8 3.5 fusion.128
  415.0 3.0 fusion.126
  426.5 3.5 fusion.128
  444.1 3.5 fusion.128
  450.3 3.0 fusion.126
  461.8 3.5 fusion.128
  468.0 3.0 fusion.126
  479.4 3.5 fusion.128
  497.1 3.5 fusion.128
  503.3 3.0 fusion.126
  512.1 70.6 %all-gather.2.cloned.1.call-done = bf16[8,32,8192]{2,1,0:T(8,128)(2,1)} async-done(((bf16[1,32,8192]{2,1,0:T(8,128)(2,1)}), bf16[8,32,8192]{2,1,0:T(8,128)(2,1)}) %all-gather.2.cloned.1.call-update) | async-done | bytes 4194320 | tf_op jit(solution)/shard_map/all_gather | solution.py:12
  587.2 40.0 %all-reduce = (f32[32,32]{1,0:T(8,128)S(1)}, f32[32,32]{1,0:T(8,128)S(1)}, f32[32,32]{1,0:T(8,128)S(1)}, f32[32,32]{1,0:T(8,128)S(1)}, f32[32,32]{1,0:T(8,128)S(1)}) all-reduce(f32[32,32]{1,0:T(8,128)S(1)} %fusion.49, f32[32,32]{1,0:T(8,128)S(1)} %convolution_bitcast_fusion.7, ...), channel_id=1, replica_groups=mesh['row'=8,'col'=4] {'row','col'}, use_global_device_ids=true, to_apply=%region_9.0 | all-reduce | flops 5120 | bytes 40960 | tf_op jit(solution)/shard_map/psum | solution.py:135
  (624 shorter events, 314.4 us)
Async XLA Ops:
  8.0 574.7 %all-gather.2.cloned.1.call-start = ((), (), s32[]{:S(2)}) async-start(), calls=%async_computation.1 | async-start | bytes 4718592 | tf_op jit(solution)/shard_map/all_gather | solution.py:12
  85.8 6.6 %copy-start.7 = (s32[64]{0:T(128)}, s32[64]{0:T(128)S(1)}, u32[]{:S(2)}) copy-start(s32[64]{0:T(128)S(1)} %get-tuple-element.318) | copy-start | bytes 772 | tf_op jit(solution)/shard_map/while
  101.1 6.6 %copy-start.7 = (s32[64]{0:T(128)}, s32[64]{0:T(128)S(1)}, u32[]{:S(2)}) copy-start(s32[64]{0:T(128)S(1)} %get-tuple-element.318) | copy-start | bytes 772 | tf_op jit(solution)/shard_map/while
  108.8 6.2 copy-start.8
  118.8 6.6 %copy-start.7 = (s32[64]{0:T(128)}, s32[64]{0:T(128)S(1)}, u32[]{:S(2)}) copy-start(s32[64]{0:T(128)S(1)} %get-tuple-element.318) | copy-start | bytes 772 | tf_op jit(solution)/shard_map/while
  126.4 6.2 copy-start.8
  136.4 6.6 %copy-start.7 = (s32[64]{0:T(128)}, s32[64]{0:T(128)S(1)}, u32[]{:S(2)}) copy-start(s32[64]{0:T(128)S(1)} %get-tuple-element.318) | copy-start | bytes 772 | tf_op jit(solution)/shard_map/while
  144.1 6.2 copy-start.8
  154.1 6.6 %copy-start.7 = (s32[64]{0:T(128)}, s32[64]{0:T(128)S(1)}, u32[]{:S(2)}) copy-start(s32[64]{0:T(128)S(1)} %get-tuple-element.318) | copy-start | bytes 772 | tf_op jit(solution)/shard_map/while
  161.7 6.2 copy-start.8
  171.7 6.6 %copy-start.7 = (s32[64]{0:T(128)}, s32[64]{0:T(128)S(1)}, u32[]{:S(2)}) copy-start(s32[64]{0:T(128)S(1)} %get-tuple-element.318) | copy-start | bytes 772 | tf_op jit(solution)/shard_map/while
  179.4 6.2 copy-start.8
  189.4 6.6 %copy-start.7 = (s32[64]{0:T(128)}, s32[64]{0:T(128)S(1)}, u32[]{:S(2)}) copy-start(s32[64]{0:T(128)S(1)} %get-tuple-element.318) | copy-start | bytes 772 | tf_op jit(solution)/shard_map/while
  197.0 6.2 copy-start.8
  207.0 6.6 %copy-start.7 = (s32[64]{0:T(128)}, s32[64]{0:T(128)S(1)}, u32[]{:S(2)}) copy-start(s32[64]{0:T(128)S(1)} %get-tuple-element.318) | copy-start | bytes 772 | tf_op jit(solution)/shard_map/while
  214.7 6.2 copy-start.8
  224.7 6.6 %copy-start.7 = (s32[64]{0:T(128)}, s32[64]{0:T(128)S(1)}, u32[]{:S(2)}) copy-start(s32[64]{0:T(128)S(1)} %get-tuple-element.318) | copy-start | bytes 772 | tf_op jit(solution)/shard_map/while
  232.3 6.2 copy-start.8
  242.3 6.6 %copy-start.7 = (s32[64]{0:T(128)}, s32[64]{0:T(128)S(1)}, u32[]{:S(2)}) copy-start(s32[64]{0:T(128)S(1)} %get-tuple-element.318) | copy-start | bytes 772 | tf_op jit(solution)/shard_map/while
  250.0 6.2 copy-start.8
  260.0 6.6 %copy-start.7 = (s32[64]{0:T(128)}, s32[64]{0:T(128)S(1)}, u32[]{:S(2)}) copy-start(s32[64]{0:T(128)S(1)} %get-tuple-element.318) | copy-start | bytes 772 | tf_op jit(solution)/shard_map/while
  267.6 6.2 copy-start.8
  277.6 6.6 %copy-start.7 = (s32[64]{0:T(128)}, s32[64]{0:T(128)S(1)}, u32[]{:S(2)}) copy-start(s32[64]{0:T(128)S(1)} %get-tuple-element.318) | copy-start | bytes 772 | tf_op jit(solution)/shard_map/while
  285.3 6.2 copy-start.8
  295.3 6.6 %copy-start.7 = (s32[64]{0:T(128)}, s32[64]{0:T(128)S(1)}, u32[]{:S(2)}) copy-start(s32[64]{0:T(128)S(1)} %get-tuple-element.318) | copy-start | bytes 772 | tf_op jit(solution)/shard_map/while
  302.9 6.2 copy-start.8
  312.9 6.6 %copy-start.7 = (s32[64]{0:T(128)}, s32[64]{0:T(128)S(1)}, u32[]{:S(2)}) copy-start(s32[64]{0:T(128)S(1)} %get-tuple-element.318) | copy-start | bytes 772 | tf_op jit(solution)/shard_map/while
  320.6 6.2 copy-start.8
  330.6 6.6 %copy-start.7 = (s32[64]{0:T(128)}, s32[64]{0:T(128)S(1)}, u32[]{:S(2)}) copy-start(s32[64]{0:T(128)S(1)} %get-tuple-element.318) | copy-start | bytes 772 | tf_op jit(solution)/shard_map/while
  338.2 6.2 copy-start.8
  348.2 6.6 %copy-start.7 = (s32[64]{0:T(128)}, s32[64]{0:T(128)S(1)}, u32[]{:S(2)}) copy-start(s32[64]{0:T(128)S(1)} %get-tuple-element.318) | copy-start | bytes 772 | tf_op jit(solution)/shard_map/while
  355.9 6.2 copy-start.8
  365.9 6.6 %copy-start.7 = (s32[64]{0:T(128)}, s32[64]{0:T(128)S(1)}, u32[]{:S(2)}) copy-start(s32[64]{0:T(128)S(1)} %get-tuple-element.318) | copy-start | bytes 772 | tf_op jit(solution)/shard_map/while
  373.5 6.2 copy-start.8
  383.5 6.6 %copy-start.7 = (s32[64]{0:T(128)}, s32[64]{0:T(128)S(1)}, u32[]{:S(2)}) copy-start(s32[64]{0:T(128)S(1)} %get-tuple-element.318) | copy-start | bytes 772 | tf_op jit(solution)/shard_map/while
  391.2 6.2 copy-start.8
  401.2 6.6 %copy-start.7 = (s32[64]{0:T(128)}, s32[64]{0:T(128)S(1)}, u32[]{:S(2)}) copy-start(s32[64]{0:T(128)S(1)} %get-tuple-element.318) | copy-start | bytes 772 | tf_op jit(solution)/shard_map/while
  408.8 6.2 copy-start.8
  418.8 6.6 %copy-start.7 = (s32[64]{0:T(128)}, s32[64]{0:T(128)S(1)}, u32[]{:S(2)}) copy-start(s32[64]{0:T(128)S(1)} %get-tuple-element.318) | copy-start | bytes 772 | tf_op jit(solution)/shard_map/while
  426.5 6.2 copy-start.8
  436.5 6.6 %copy-start.7 = (s32[64]{0:T(128)}, s32[64]{0:T(128)S(1)}, u32[]{:S(2)}) copy-start(s32[64]{0:T(128)S(1)} %get-tuple-element.318) | copy-start | bytes 772 | tf_op jit(solution)/shard_map/while
  444.1 6.2 copy-start.8
  454.1 6.6 %copy-start.7 = (s32[64]{0:T(128)}, s32[64]{0:T(128)S(1)}, u32[]{:S(2)}) copy-start(s32[64]{0:T(128)S(1)} %get-tuple-element.318) | copy-start | bytes 772 | tf_op jit(solution)/shard_map/while
  461.8 6.2 copy-start.8
  471.8 6.6 %copy-start.7 = (s32[64]{0:T(128)}, s32[64]{0:T(128)S(1)}, u32[]{:S(2)}) copy-start(s32[64]{0:T(128)S(1)} %get-tuple-element.318) | copy-start | bytes 772 | tf_op jit(solution)/shard_map/while
  489.4 6.6 %copy-start.7 = (s32[64]{0:T(128)}, s32[64]{0:T(128)S(1)}, u32[]{:S(2)}) copy-start(s32[64]{0:T(128)S(1)} %get-tuple-element.318) | copy-start | bytes 772 | tf_op jit(solution)/shard_map/while
  508.7 76.9 %all-reduce.3.cloned.1.call-start = ((), (), s32[]{:S(2)}) async-start(), calls=%async_computation | async-start | bytes 524288 | tf_op jit(solution)/shard_map/psum | solution.py:126
  511.7 131.0 %copy-start.9 = (f32[32,1024]{1,0:T(8,128)S(1)}, f32[32,1024]{1,0:T(8,128)}, u32[]{:S(2)}) copy-start(f32[32,1024]{1,0:T(8,128)} %param.13) | copy-start | bytes 393220
  (103 other events, 289.7 us)
Sparse Core Ops, SparseCore 0:
  508.8 73.8 all-gather.1
Sparse Core Ops, SparseCore 1:
  511.5 33.0 all-reduce.2
